TPU v7x, 32 devices: a whole 2x2x4 slice. The times are simulated.
32 devices in a mesh: dp: 4 (over z), ctx: 8 (over y, x, core).
Axes of the slice: x: 2, y: 2, z: 4, core: 2. Of those that a mesh axis runs over, the one named last changes fastest.
Arguments:
- queries: bfloat16 [4, 1024, 2048], P('dp', 'ctx'), may hold values from -6 to 6
- keys: bfloat16 [4, 1024, 2048], P('dp', 'ctx'), may hold values from -6 to 6
- values: bfloat16 [4, 1024, 2048], P('dp', 'ctx'), may hold values from -6 to 6
- prior_state: float32 [4, 16, 128, 128], P('dp'), may hold values from -96 to 96
- norm_gain: float32 [2048], replicated, may hold values from 0.1 to 1.9
- router_weight: bfloat16 [2048, 32], replicated, may hold values from -0.125 to 0.125
- expert_ids: int32 [4, 1024, 4], P('dp', 'ctx'), may hold values from 0 to 31, all different within a row; in each aligned block of 128 rows (0 to 127, 128 to 255, ..., all dimensions but the last counted through in order) at most 24 rows name the same one
- w_gate: bfloat16 [32, 2048, 768], P(('dp', 'ctx')), may hold values from -0.125 to 0.125
- w_up: bfloat16 [32, 2048, 768], P(('dp', 'ctx')), may hold values from -0.125 to 0.125
- w_down: bfloat16 [32, 768, 2048], P(('dp', 'ctx')), may hold values from -0.21875 to 0.21875
- cotangent: bfloat16 [4, 1024, 2048], P('dp', 'ctx'), may hold values from -6 to 6
Outputs:
- output: bfloat16 [4, 1024, 2048], P('dp', 'ctx')
- grad_queries: bfloat16 [4, 1024, 2048], P('dp', 'ctx')
- grad_keys: bfloat16 [4, 1024, 2048], P('dp', 'ctx')
- grad_values: bfloat16 [4, 1024, 2048], P('dp', 'ctx')
- grad_gate: bfloat16 [32, 2048, 768], P(('dp', 'ctx'))
- grad_up: bfloat16 [32, 2048, 768], P(('dp', 'ctx'))
- grad_down: bfloat16 [32, 768, 2048], P(('dp', 'ctx'))
- grad_router: float32 [2048, 32], replicated
Inputs may be any that keep to these rules, and one draw needn't show every extreme that they name: `expert_ids`: within the rows of one device (aligned blocks of 128 tokens) no expert is named more than 24 times, and in every draw some expert is named exactly 24 times there; the 4 ids of one token differ.
All inputs are finite; a program needn't handle non-finite values.
Results may differ from a plain program's by a relative error of at most 0.012.
Values may be sent and summed in bfloat16 or wider, within the bound.
No kernel may reach another device: no remote copies, remote signals or barrier semaphores. Data moves between devices by JAX's collectives and lax.ppermute only.
A program may use at most 192 MiB of HBM per device.

v0:
```python
import jax
import jax.numpy as jnp
from jax import lax
from jax.sharding import PartitionSpec as P

H = 16
DH = 128
D = 2048
TOPK = 4
epsilon = 1e-05
exact_mode = lax.Precision.HIGHEST


def carried_in(value, axis, join, neutral):
    count, mine = (lax.axis_size(axis), lax.axis_index(axis))
    pieces = lax.all_gather(value, axis)
    total = jnp.full_like(value, 0) + jnp.asarray(neutral, value.dtype)

    def step(position, total):
        longer = join(total, pieces[position])
        return jnp.where(position < mine, longer, total)

    return lax.fori_loop(0, count - 1, step, total)


def entering(value, axis, join, neutral):
    count = lax.axis_size(axis)
    place = lax.axis_index(axis)
    ahead = count - 1 - place
    gathered = lax.all_gather(value.astype(jnp.bfloat16), axis)
    state = jnp.zeros_like(value) + jnp.asarray(neutral, value.dtype)

    def one(step, state):
        source = count - 1 - step
        return join(state, lax.dynamic_index_in_dim(gathered, source, 0, False).astype(value.dtype))

    return lax.fori_loop(0, ahead, one, state)


def add_states(earlier, later):
    return earlier + later


def expert_forward(inputs, gate_mat, up_mat, down_mat):
    gate_pre = jnp.dot(inputs, gate_mat, preferred_element_type=jnp.float32)
    up_pre = jnp.dot(inputs, up_mat, preferred_element_type=jnp.float32)
    gate_sig = jax.nn.sigmoid(gate_pre)
    hidden = (gate_pre * gate_sig * up_pre).astype(jnp.bfloat16)
    produced = jnp.dot(hidden, down_mat, preferred_element_type=jnp.float32).astype(jnp.bfloat16)
    return (gate_pre, up_pre, gate_sig, hidden, produced)


def expert_backward(
    inputs, grad_out, gate_pre, up_pre, gate_sig, hidden, gate_mat, up_mat, down_mat
):
    grad_hidden = jnp.dot(grad_out, down_mat.T, preferred_element_type=jnp.float32)
    grad_gate_pre = (grad_hidden * up_pre * gate_sig * (1.0 + gate_pre * (1.0 - gate_sig))).astype(
        jnp.bfloat16
    )
    grad_up_pre = (grad_hidden * gate_pre * gate_sig).astype(jnp.bfloat16)
    grad_down = jnp.dot(hidden.T, grad_out, preferred_element_type=jnp.float32).astype(jnp.bfloat16)
    grad_gate = jnp.dot(inputs.T, grad_gate_pre, preferred_element_type=jnp.float32).astype(
        jnp.bfloat16
    )
    grad_up = jnp.dot(inputs.T, grad_up_pre, preferred_element_type=jnp.float32).astype(
        jnp.bfloat16
    )
    grad_inputs = (
        jnp.dot(grad_gate_pre, gate_mat.T, preferred_element_type=jnp.float32)
        + jnp.dot(grad_up_pre, up_mat.T, preferred_element_type=jnp.float32)
    ).astype(jnp.bfloat16)
    return (grad_inputs, grad_gate, grad_up, grad_down)


def slot_layout(flat_ids, experts_all, capacity):
    count_assign = flat_ids.shape[0]
    onehot = (flat_ids[:, None] == jnp.arange(experts_all, dtype=jnp.int32)[None, :]).astype(
        jnp.int32
    )
    before = jnp.cumsum(onehot, axis=0) - onehot
    slot_rank = jnp.sum(before * onehot, axis=1)
    slot_index = flat_ids * capacity + slot_rank
    source = (
        jnp.full((experts_all * capacity,), -1, jnp.int32)
        .at[slot_index]
        .set(jnp.arange(count_assign, dtype=jnp.int32))
    )
    return (slot_index, source)


def route_rows(block):
    return lax.all_to_all(block, ("dp", "ctx"), split_axis=0, concat_axis=0, tiled=True)


def local(
    queries,
    keys,
    values,
    prior_state,
    norm_gain,
    router_weight,
    expert_ids,
    w_gate,
    w_up,
    w_down,
    cotangent,
):
    token_count = queries.shape[1]
    experts_all = router_weight.shape[1]
    capacity = max(2, 3 * token_count * TOPK // (2 * experts_all))
    queries3 = queries[0].reshape(token_count, H, DH)
    keys3 = keys[0].reshape(token_count, H, DH)
    values3 = values[0].reshape(token_count, H, DH)
    state_term = jnp.einsum("shi,shj->hij", keys3, values3, preferred_element_type=jnp.float32)
    zero_state = jnp.zeros_like(state_term)
    earlier_states = carried_in(state_term, "ctx", add_states, zero_state)
    state_in = prior_state[0] + earlier_states
    causal = jnp.arange(token_count)[:, None] >= jnp.arange(token_count)[None, :]
    scores = jnp.einsum("thd,shd->hts", queries3, keys3, preferred_element_type=jnp.float32)
    attn_scores = jnp.where(causal[None], scores, 0.0).astype(jnp.bfloat16)
    intra = jnp.einsum("hts,shj->thj", attn_scores, values3, preferred_element_type=jnp.float32)
    inter = jnp.einsum("thi,hij->thj", queries3.astype(jnp.float32), state_in, precision=exact_mode)
    attended = intra + inter
    gain_heads = norm_gain.reshape(H, DH)
    mean_square = jnp.mean(attended * attended, axis=-1, keepdims=True)
    scale_root = jnp.sqrt(mean_square + epsilon)
    mixed_rows = (attended / scale_root * gain_heads).astype(jnp.bfloat16).reshape(token_count, D)
    logits = jnp.dot(mixed_rows, router_weight, preferred_element_type=jnp.float32)
    token_ids = expert_ids[0]
    onehot_sel = (
        token_ids[:, :, None] == jnp.arange(experts_all, dtype=jnp.int32)[None, None, :]
    ).astype(jnp.float32)
    selected = jnp.sum(logits[:, None, :] * onehot_sel, axis=-1)
    gate_sig_r = jax.nn.sigmoid(selected)
    sig_total = jnp.sum(gate_sig_r, axis=1, keepdims=True)
    gates = gate_sig_r / sig_total
    slot_index, source = slot_layout(token_ids.reshape(-1), experts_all, capacity)
    filled = source >= 0
    row_of = jnp.where(filled, source // TOPK, 0)
    send_block = jnp.where(
        filled[:, None], mixed_rows[row_of], jnp.zeros((), jnp.bfloat16)
    ).reshape(experts_all, capacity, D)
    grad_y = cotangent[0].astype(jnp.float32)
    grad_out_assign = (
        (gates[:, :, None] * grad_y[:, None, :]).astype(jnp.bfloat16).reshape(token_count * TOPK, D)
    )
    send_grad = jnp.where(
        filled[:, None], grad_out_assign[jnp.where(filled, source, 0)], jnp.zeros((), jnp.bfloat16)
    ).reshape(experts_all, capacity, D)
    gate_mat = w_gate[0]
    up_mat = w_up[0]
    down_mat = w_down[0]
    received = route_rows(send_block).reshape(-1, D)
    gate_pre, up_pre, gate_sig, hidden, produced = expert_forward(
        received, gate_mat, up_mat, down_mat
    )
    returned = route_rows(produced.reshape(experts_all, capacity, D)).reshape(-1, D)
    received_grad = route_rows(send_grad).reshape(-1, D)
    grad_inputs, grad_gate, grad_up, grad_down = expert_backward(
        received, received_grad, gate_pre, up_pre, gate_sig, hidden, gate_mat, up_mat, down_mat
    )
    returned_grad = route_rows(grad_inputs.reshape(experts_all, capacity, D)).reshape(-1, D)
    out_float = returned[slot_index].reshape(token_count, TOPK, D).astype(jnp.float32)
    moe_sum = jnp.sum(gates[:, :, None] * out_float, axis=1)
    output = (mixed_rows.astype(jnp.float32) + moe_sum).astype(jnp.bfloat16)
    grad_gates = jnp.sum(out_float * grad_y[:, None, :], axis=-1)
    grad_assign = returned_grad[slot_index].reshape(token_count, TOPK, D).astype(jnp.float32)
    grad_moe = jnp.sum(gates[:, :, None] * grad_assign, axis=1)
    weighted_sum = jnp.sum(gates * grad_gates, axis=1, keepdims=True)
    grad_selected = gate_sig_r * (1.0 - gate_sig_r) * (grad_gates - weighted_sum) / sig_total
    grad_logits = jnp.sum(grad_selected[:, :, None] * onehot_sel, axis=1)
    router_term = jnp.dot(mixed_rows.astype(jnp.float32).T, grad_logits, precision=exact_mode)
    grad_router = lax.psum(router_term, ("dp", "ctx"))
    router_back = jnp.dot(grad_logits, router_weight.astype(jnp.float32).T, precision=exact_mode)
    grad_mixed = grad_y + grad_moe + router_back
    weighted = gain_heads * grad_mixed.reshape(token_count, H, DH)
    inner = jnp.sum(weighted * attended, axis=-1, keepdims=True)
    grad_attended = (
        (weighted - attended * (inner / (DH * (mean_square + epsilon)))) / scale_root
    ).astype(jnp.bfloat16)
    grad_term = jnp.einsum(
        "thi,thj->hij", queries3, grad_attended, preferred_element_type=jnp.float32
    )
    later_states = entering(grad_term, "ctx", add_states, zero_state)
    grad_scores = jnp.where(
        causal[None],
        jnp.einsum("thj,shj->hts", grad_attended, values3, preferred_element_type=jnp.float32),
        0.0,
    ).astype(jnp.bfloat16)
    grad_q = jnp.einsum(
        "hts,shi->thi", grad_scores, keys3, preferred_element_type=jnp.float32
    ) + jnp.einsum(
        "thj,hij->thi", grad_attended.astype(jnp.float32), state_in, precision=exact_mode
    )
    grad_k = jnp.einsum(
        "hts,thi->shi", grad_scores, queries3, preferred_element_type=jnp.float32
    ) + jnp.einsum("shj,hij->shi", values3.astype(jnp.float32), later_states, precision=exact_mode)
    grad_v = jnp.einsum(
        "hts,thj->shj", attn_scores, grad_attended, preferred_element_type=jnp.float32
    ) + jnp.einsum("shi,hij->shj", keys3.astype(jnp.float32), later_states, precision=exact_mode)
    row_shape = (1, token_count, D)
    return (
        output.reshape(row_shape),
        grad_q.astype(jnp.bfloat16).reshape(row_shape),
        grad_k.astype(jnp.bfloat16).reshape(row_shape),
        grad_v.astype(jnp.bfloat16).reshape(row_shape),
        grad_gate[None],
        grad_up[None],
        grad_down[None],
        grad_router,
    )


def solution(mesh):
    placed = (
        P("dp", "ctx", None),
        P("dp", "ctx", None),
        P("dp", "ctx", None),
        P("dp", None, None, None),
        P(),
        P(),
        P("dp", "ctx", None),
        P(("dp", "ctx"), None, None),
        P(("dp", "ctx"), None, None),
        P(("dp", "ctx"), None, None),
        P("dp", "ctx", None),
    )
    return jax.shard_map(
        local,
        mesh=mesh,
        in_specs=placed,
        out_specs=(
            P("dp", "ctx", None),
            P("dp", "ctx", None),
            P("dp", "ctx", None),
            P("dp", "ctx", None),
            P(("dp", "ctx"), None, None),
            P(("dp", "ctx"), None, None),
            P(("dp", "ctx"), None, None),
            P(),
        ),
        check_vma=False,
    )
```

profile of v0, /device:TPU:0, one launch (start us, length us, event | category | flops | bytes accessed | tf_op | source)
XLA Modules:
  0.0 655.8 jit_solution(7271364659372480334)
XLA Ops:
  7.2 2.1 copy.168
  9.3 2.2 copy.134
  13.5 2.3 fusion.28
  20.3 3.1 mul.169
  23.4 5.5 mul.170
  30.7 2.4 scatter_custom_fusion
  33.3 2.5 fusion.17
  35.8 37.3 %all-gather.5.cloned.1.call-done = f32[128,128,128]{2,1,0:T(8,128)} async-done(((f32[16,128,128]{2,1,0:T(8,128)}), f32[128,128,128]{2,1,0:T(8,128)}) %all-gather.5.cloned.1.call-update) | async-done | bytes 8388624 | tf_op jit(solution)/shard_map/all_gather | solution.py:16
  73.1 18.7 %while.27 = (s32[]{:T(128)}, f32[16,128,128]{2,1,0:T(8,128)}, s32[]{:T(128)}, f32[8,16,128,128]{3,2,1,0:T(8,128)}, s32[]{:T(128)}, /*index=5*/s32[]{:T(128)}) while((s32[]{:T(128)}, f32[16,128,128]{2,1,0:T(8,128)}, s32[]{:T(128)}, f32[8,16,128,128]{3,2,1,0:T(8,128)}, s32[]{:T(128)}, /*index=5*/s32[]{:T(128)}) %tuple.85), condition=%wide.region_1.2_spmd.clone, body=%wide.region_0.1_spmd.clone.sunk | while | flops 786436 | bytes 3145821 | solution.py:23
  73.1 2.4 add_select_fusion.3
  75.5 2.7 add_select_fusion.3
  78.2 2.7 add_select_fusion.3
  80.9 2.7 add_select_fusion.3
  83.7 2.7 add_select_fusion.3
  86.4 2.7 add_select_fusion.3
  89.1 2.7 add_select_fusion.3
  91.8 2.8 convolution_bitcast_fusion.5
  100.9 3.8 multiply_convert_fusion
  104.7 8.9 %gather_fusion.2 = bf16[768,2048]{1,0:T(8,128)(2,1)} fusion(bf16[512,2048]{1,0:T(8,128)(2,1)} %multiply_convert_fusion, s32[1024]{0:T(1024)S(1)} %get-tuple-element.236), kind=kCustom, calls=%fused_computation.2 | custom fusion | bytes 6294528 | tf_op jit(solution)/shard_map/gather | solution.py:148
  113.6 8.2 %gather_fusion = bf16[768,2048]{1,0:T(8,128)(2,1)} fusion(bf16[128,2048]{1,0:T(8,128)(2,1)} %copy.143, s32[1024]{0:T(1024)S(1)} %get-tuple-element.237), kind=kCustom, calls=%fused_computation | custom fusion | bytes 6294528 | tf_op jit(solution)/shard_map/gather | solution.py:141
  121.8 4.3 broadcast_select_fusion
  126.1 76.1 %all_to_all.20 = bf16[32,24,2048]{2,1,0:T(8,128)(2,1)} all-to-all(bf16[32,24,2048]{2,1,0:T(8,128)(2,1)S(1)} %get-tuple-element.231), channel_id=1, replica_groups=mesh['dp'=4,'ctx'=8] {'dp','ctx'}, dimensions={0} | all-to-all | bytes 6291456 | tf_op jit(solution)/shard_map/all_to_all | solution.py:92
  202.2 3.8 all-to-all-start.2
  206.0 7.0 %fusion.4 = f32[768,768]{1,0:T(8,128)} fusion(bf16[768,2048]{1,0:T(8,128)(2,1)} %bitcast.170, bf16[1,2048,768]{2,1,0:T(8,128)(2,1)} %param.23), kind=kOutput, calls=%fused_computation.20 | convolution fusion | flops 2415919104 | bytes 8650752 | tf_op jit(solution)/shard_map/dot_general | solution.py:46
  213.0 4.0 fusion.8
  217.1 60.4 %all-to-all-done.2 = bf16[32,24,2048]{2,1,0:T(8,128)(2,1)} async-done(((bf16[32,24,2048]{2,1,0:T(8,128)(2,1)}), bf16[32,24,2048]{2,1,0:T(8,128)(2,1)}, u32[]{:S(2)}, u32[]{:S(2)}) %all-to-all-start.2) | async-done | bytes 3145760 | tf_op jit(solution)/shard_map/all_to_all | solution.py:92
  277.5 7.9 %multiply_convert_fusion.1 = (bf16[768,768]{1,0:T(8,128)(2,1)S(1)}, bf16[768,768]{1,0:T(8,128)(2,1)S(1)}, bf16[768,768]{1,0:T(8,128)(2,1)}) fusion(f32[768,768]{1,0:T(8,128)} %fusion.8, f32[768,768]{1,0:T(8,128)} %fusion.4, bf16[768,2048]{1,0:T(8,128)(2,1)} %bitcast.23, bf16[1,768,2048]{2,1,0:T(8,128)(2,1)S(1)} %copy-done), kind=kOutput, calls=%fused_computation.32 | convolution fusion | flops 2425356288 | bytes 14548992 | tf_op jit(solution)/shard_map/dot_general | solution.py:56
  285.4 2.6 fusion.6
  288.1 4.0 add_convert_fusion
  292.1 4.0 all-to-all-start.3
  296.1 5.2 convolution_convert_fusion.3
  301.3 66.2 %all-to-all-done.3 = bf16[32,24,2048]{2,1,0:T(8,128)(2,1)} async-done(((bf16[32,24,2048]{2,1,0:T(8,128)(2,1)}), bf16[32,24,2048]{2,1,0:T(8,128)(2,1)}, u32[]{:S(2)}, u32[]{:S(2)}) %all-to-all-start.3) | async-done | bytes 3145760 | tf_op jit(solution)/shard_map/all_to_all | solution.py:92
  367.6 4.0 all-to-all-start.1
  371.9 7.5 %gather_fusion.3 = bf16[512,2048]{1,0:T(8,128)(2,1)} fusion(bf16[768,2048]{1,0:T(8,128)(2,1)} %bitcast.25, s32[1024]{0:T(1024)S(1)} %pad_clamp_fusion.1), kind=kCustom, calls=%fused_computation.3 | custom fusion | bytes 4196352 | tf_op jit(solution)/shard_map/gather | solution.py:167
  379.4 4.7 reshape.283
  384.1 59.0 %all-to-all-done.1 = bf16[32,24,2048]{2,1,0:T(8,128)(2,1)} async-done(((bf16[32,24,2048]{2,1,0:T(8,128)(2,1)}), bf16[32,24,2048]{2,1,0:T(8,128)(2,1)}, u32[]{:S(2)}, u32[]{:S(2)}) %all-to-all-start.1) | async-done | bytes 3145760 | tf_op jit(solution)/shard_map/all_to_all | solution.py:92
  443.1 7.5 %gather_fusion.1 = bf16[512,2048]{1,0:T(8,128)(2,1)} fusion(bf16[768,2048]{1,0:T(8,128)(2,1)} %bitcast.18, s32[1024]{0:T(1024)S(1)} %pad_clamp_fusion.1), kind=kCustom, calls=%fused_computation.1 | custom fusion | bytes 4196352 | tf_op jit(solution)/shard_map/gather | solution.py:163
  450.6 4.7 reshape.279
  455.4 11.2 %multiply_reduce_fusion = (f32[128,4]{1,0:T(8,128)S(1)}, f32[128,2048]{1,0:T(8,128)}, f32[128,2048]{1,0:T(8,128)}) fusion(f32[128,4,2048]{2,1,0:T(4,128)} %reshape.279, f32[128,2048]{1,0:T(8,128)} %copy-done.4, f32[128,4]{1,0:T(8,128)S(1)} %copy.138, f32[128,4,2048]{2,1,0:T(4,128)} %reshape.283), kind=kLoop, calls=%fused_computation.8 | loop fusion | flops 5766656 | bytes 11538432 | tf_op jit(solution)/shard_map/reduce_sum | solution.py:166
  466.7 3.0 convolution_add_fusion
  469.6 2.5 copy.148
  480.3 2.1 bitcast_convert_fusion
  482.4 2.5 copy.144
  484.9 7.0 %fusion.10 = bf16[1,2048,768]{2,1,0:T(8,128)(2,1)} fusion(bf16[768,2048]{1,0:T(8,128)(2,1)} %bitcast.171, bf16[768,768]{1,0:T(8,128)(2,1)} %copy-done.26), kind=kOutput, calls=%fused_computation.28 | convolution fusion | flops 2417491968 | bytes 7471104 | tf_op jit(solution)/shard_map/dot_general | solution.py:62
  491.9 4.1 fusion.11
  496.0 6.1 fusion.12
  504.6 2.0 copy.159
  506.7 2.4 fusion.49
  509.1 2.5 fusion.48
  511.6 2.5 fusion.22
  514.0 2.2 all-gather.7.cloned.1.call-done
  517.3 17.3 %while.26 = (s32[]{:T(128)}, f32[16,128,128]{2,1,0:T(8,128)}, s32[]{:T(128)}, bf16[8,16,128,128]{3,2,1,0:T(8,128)(2,1)}, s32[]{:T(128)}, /*index=5*/s32[]{:T(128)}, s32[]{:T(128)}, s32[]{:T(128)}) while((s32[]{:T(128)}, f32[16,128,128]{2,1,0:T(8,128)}, s32[]{:T(128)}, bf16[8,16,128,128]{3,2,1,0:T(8,128)(2,1)}, s32[]{:T(128)}, ...), condition=%wide.region_16.17_spmd, body=%wide.region_15.16_spmd.sunk | while | flops 524294 | bytes 2621575 | solution.py:37
  517.3 2.5 convert_add_fusion.2
  519.8 2.5 convert_add_fusion.2
  522.3 2.5 convert_add_fusion.2
  524.8 2.5 convert_add_fusion.2
  527.2 2.5 convert_add_fusion.2
  529.7 2.5 convert_add_fusion.2
  532.2 2.5 convert_add_fusion.2
  534.7 2.7 convolution_bitcast_fusion.3
  537.4 2.9 fusion.16
  541.4 2.0 copy.161
  543.5 2.0 copy.160
  545.5 101.8 %all-reduce.2.cloned.1.call-done = f32[2048,32]{0,1:T(8,128)} async-done(((f32[2048,32]{0,1:T(8,128)}), f32[2048,32]{0,1:T(8,128)}) %all-reduce.2.cloned.1.call-update) | async-done | bytes 262160 | tf_op jit(solution)/shard_map/psum | solution.py:173
  (115 shorter events, 29.5 us)
Async XLA Ops:
  7.2 270.3 %copy-start = (bf16[1,768,2048]{2,1,0:T(8,128)(2,1)S(1)}, bf16[1,768,2048]{2,1,0:T(8,128)(2,1)}, u32[]{:S(2)}) copy-start(bf16[1,768,2048]{2,1,0:T(8,128)(2,1)} %param.24) | copy-start | bytes 9437188
  7.2 65.9 %all-gather.5.cloned.1.call-start = ((), (), s32[]{:S(2)}) async-start(), calls=%async_computation.5 | async-start | bytes 9437184 | tf_op jit(solution)/shard_map/all_gather | solution.py:16
  7.2 8.7 %copy-start.22 = (s32[1,128,4]{1,2,0:T(4,128)S(1)}, s32[1,128,4]{1,2,0:T(4,128)}, u32[]{:S(2)}) copy-start(s32[1,128,4]{1,2,0:T(4,128)} %param.21) | copy-start | bytes 6148
  12.7 0.8 copy-start.9
  19.3 1.0 copy-start.4
  91.8 2.8 copy-start.10
  91.8 2.8 copy-start.19
  91.8 4.3 copy-start.21
  94.6 4.7 copy-start.20
  95.2 1.0 copy-start.3
  202.2 75.2 %all-to-all-start.2 = ((bf16[32,24,2048]{2,1,0:T(8,128)(2,1)}), bf16[32,24,2048]{2,1,0:T(8,128)(2,1)}, u32[]{:S(2)}, u32[]{:S(2)}) async-start(bf16[32,24,2048]{2,1,0:T(8,128)(2,1)} %get-tuple-element.230), calls=%async_computation.2 | async-start | bytes 6291456 | tf_op jit(solution)/shard_map/all_to_all | solution.py:92
  206.0 7.0 %copy-start.15 = (bf16[32,24,2048]{2,1,0:T(8,128)(2,1)S(1)}, bf16[32,24,2048]{2,1,0:T(8,128)(2,1)}, u32[]{:S(2)}) copy-start(bf16[32,24,2048]{2,1,0:T(8,128)(2,1)} %all_to_all.20) | copy-start | bytes 9437188
  206.0 7.0 %copy-start.23 = (bf16[1,2048,768]{2,1,0:T(8,128)(2,1)S(1)}, bf16[1,2048,768]{2,1,0:T(8,128)(2,1)}, u32[]{:S(2)}) copy-start(bf16[1,2048,768]{2,1,0:T(8,128)(2,1)} %param.22) | copy-start | bytes 9437188
  277.5 7.9 %copy-start.24 = (bf16[1,2048,768]{2,1,0:T(8,128)(2,1)S(1)}, bf16[1,2048,768]{2,1,0:T(8,128)(2,1)}, u32[]{:S(2)}) copy-start(bf16[1,2048,768]{2,1,0:T(8,128)(2,1)} %param.22) | copy-start | bytes 9437188
  285.3 2.7 copy-start.26
  285.3 2.7 copy-start.28
  285.3 2.7 copy-start.25
  292.1 75.5 %all-to-all-start.3 = ((bf16[32,24,2048]{2,1,0:T(8,128)(2,1)}), bf16[32,24,2048]{2,1,0:T(8,128)(2,1)}, u32[]{:S(2)}, u32[]{:S(2)}) async-start(bf16[32,24,2048]{2,1,0:T(8,128)(2,1)} %bitcast.175), calls=%async_computation.3 | async-start | bytes 6291456 | tf_op jit(solution)/shard_map/all_to_all | solution.py:92
  367.6 75.5 %all-to-all-start.1 = ((bf16[32,24,2048]{2,1,0:T(8,128)(2,1)}), bf16[32,24,2048]{2,1,0:T(8,128)(2,1)}, u32[]{:S(2)}, u32[]{:S(2)}) async-start(bf16[32,24,2048]{2,1,0:T(8,128)(2,1)} %bitcast.174), calls=%async_computation.1 | async-start | bytes 6291456 | tf_op jit(solution)/shard_map/all_to_all | solution.py:92
  371.6 144.6 %all-gather.7.cloned.1.call-start = ((), (), s32[]{:S(2)}) async-start(), calls=%async_computation.6 | async-start | bytes 4718592 | tf_op jit(solution)/shard_map/all_gather | solution.py:30
  472.2 4.7 copy-start.5
  476.0 0.8 copy-start.7
  480.0 167.3 %all-reduce.2.cloned.1.call-start = ((), (), s32[]{:S(2)}) async-start(), calls=%async_computation.4 | async-start | bytes 524288 | tf_op jit(solution)/shard_map/psum | solution.py:173
  484.9 7.0 %copy-start.16 = (bf16[32,24,2048]{2,1,0:T(8,128)(2,1)S(1)}, bf16[32,24,2048]{2,1,0:T(8,128)(2,1)}, u32[]{:S(2)}) copy-start(bf16[32,24,2048]{2,1,0:T(8,128)(2,1)} %all_to_all.20) | copy-start | bytes 9437188
  484.9 7.0 %copy-start.29 = (bf16[768,768]{1,0:T(8,128)(2,1)S(1)}, bf16[768,768]{1,0:T(8,128)(2,1)}, u32[]{:S(2)}) copy-start(bf16[768,768]{1,0:T(8,128)(2,1)} %copy-done.28) | copy-start | bytes 3538948
  491.9 4.1 copy-start.27
  496.0 6.1 copy-start.8
  496.0 6.1 copy-start.11
  496.0 6.6 %copy-start.2 = (f32[16,128,128]{2,1,0:T(8,128)S(1)}, f32[16,128,128]{2,1,0:T(8,128)}, u32[]{:S(2)}) copy-start(f32[16,128,128]{2,1,0:T(8,128)} %get-tuple-element.143) | copy-start | bytes 3145732
  496.0 6.6 %copy-start.13 = (f32[1,16,128,128]{3,2,1,0:T(8,128)S(1)}, f32[1,16,128,128]{3,2,1,0:T(8,128)}, u32[]{:S(2)}) copy-start(f32[1,16,128,128]{3,2,1,0:T(8,128)} %param.18) | copy-start | bytes 3145732
  502.1 1.2 copy-start.12
  502.6 2.0 copy-start.17
  534.7 2.7 copy-start.1
  534.7 2.8 copy-start.14
  534.7 5.6 copy-start.6
  534.7 5.6 copy-start.18
Sparse Core Ops, SparseCore 0:
  16.0 57.0 all-gather.4
  480.1 36.0 all-gather.6
  522.3 124.9 all-reduce.1
where the time goes:
time: 666 us; the launch traced here: 656 us
  waiting for transfers between devices  327 us (49%)
  local copies, waits for them, and re-layouts  83.1 us (12%)
  blocking collectives  76.1 us (11%)
  matrix products  75.4 us (11%)
  other arithmetic  67.4 us (10%)
  between operations  14.4 us (2%)
  starting transfers between devices  12.4 us (2%)
    all_to_all x3, waiting for transfers between devices, route_rows(): lax.all_to_all(block, ('dp', 'ctx'), split_axis=0, concat_axis=0, tiled=T...  186 us
    psum x1, waiting for transfers between devices, local(): grad_router = lax.psum(router_term, ('dp', 'ctx'))  102 us
    all_to_all x1, blocking collectives, route_rows(): lax.all_to_all(block, ('dp', 'ctx'), split_axis=0, concat_axis=0, tiled=T...  76.1 us
    all_gather x1, waiting for transfers between devices, carried_in(): pieces = lax.all_gather(value, axis)  37.3 us
    select_n x7, other arithmetic, step(): return jnp.where(position < mine, longer, total)  18.7 us
    add x7, other arithmetic, add_states(): return earlier + later  17.3 us
    unnamed x68, local copies, waits for them, and re-layouts  16.8 us
  transfers between devices with their start and end apart: 6, of which 6 were waited for; matrix products, arithmetic and copies ran while one was open for 17% of the time, Pallas kernels for 0%

commit v1 on v0

--- a/solution.py
+++ b/solution.py
@@ -170,7 +170,7 @@
     grad_selected = gate_sig_r * (1.0 - gate_sig_r) * (grad_gates - weighted_sum) / sig_total
     grad_logits = jnp.sum(grad_selected[:, :, None] * onehot_sel, axis=1)
     router_term = jnp.dot(mixed_rows.astype(jnp.float32).T, grad_logits, precision=exact_mode)
-    grad_router = lax.psum(router_term, ("dp", "ctx"))
+    grad_router = lax.psum(lax.psum(router_term, "ctx"), "dp")
     router_back = jnp.dot(grad_logits, router_weight.astype(jnp.float32).T, precision=exact_mode)
     grad_mixed = grad_y + grad_moe + router_back
     weighted = gain_heads * grad_mixed.reshape(token_count, H, DH)

time: 666 us -> 627 us (0.941)
  waiting for transfers between devices: 327 us -> 284 us
    psum x1 -> x2, waiting for transfers between devices: 102 us -> 23.2 us  [local(): grad_router = lax.psum(lax.psum(router_term, 'ctx'), 'dp')]
    all_gather x1, waiting for transfers between devices: 2.22 us -> 38.2 us  [entering(): gathered = lax.all_gather(value.astype(jnp.bfloat16), axis)]
    unnamed x68 -> x60, local copies, waits for them, and re-layouts: 16.8 us -> 16 us
  transfers between devices with their start and end apart: 6 -> 7, of which waited for: 6 -> 7; matrix products, arithmetic and copies ran while one was open for 17% -> 19% of each run, Pallas kernels for 0% -> 0%
where the time goes in v1:
time: 627 us; the launch traced here: 616 us
  waiting for transfers between devices  284 us (45%)
  local copies, waits for them, and re-layouts  82.3 us (13%)
  matrix products  78.7 us (13%)
  blocking collectives  76.1 us (12%)
  other arithmetic  68.1 us (11%)
  between operations  14.4 us (2%)
  starting transfers between devices  12.4 us (2%)
    all_to_all x3, waiting for transfers between devices, route_rows(): lax.all_to_all(block, ('dp', 'ctx'), split_axis=0, concat_axis=0, tiled=T...  186 us
    all_to_all x1, blocking collectives, route_rows(): lax.all_to_all(block, ('dp', 'ctx'), split_axis=0, concat_axis=0, tiled=T...  76.1 us
    all_gather x1, waiting for transfers between devices, entering(): gathered = lax.all_gather(value.astype(jnp.bfloat16), axis)  38.2 us
    all_gather x1, waiting for transfers between devices, carried_in(): pieces = lax.all_gather(value, axis)  37.3 us
    psum x2, waiting for transfers between devices, local(): grad_router = lax.psum(lax.psum(router_term, 'ctx'), 'dp')  23.2 us
    select_n x7, other arithmetic, step(): return jnp.where(position < mine, longer, total)  18.6 us
    add x7, other arithmetic, add_states(): return earlier + later  17.3 us
    unnamed x60, local copies, waits for them, and re-layouts  16 us
  transfers between devices with their start and end apart: 7, of which 7 were waited for; matrix products, arithmetic and copies ran while one was open for 19% of the time, Pallas kernels for 0%

profile of v1, /device:TPU:0, one launch (start us, length us, event | category | flops | bytes accessed | tf_op | source)
XLA Modules:
  0.0 616.3 jit_solution(11355157116386442579)
XLA Ops:
  7.2 2.1 copy.168
  9.3 2.2 copy.134
  13.5 2.3 fusion.28
  20.3 3.1 mul.169
  23.4 5.5 mul.170
  30.7 2.4 scatter_custom_fusion
  33.3 2.5 fusion.17
  35.8 37.3 %all-gather.5.cloned.1.call-done = f32[128,128,128]{2,1,0:T(8,128)} async-done(((f32[16,128,128]{2,1,0:T(8,128)}), f32[128,128,128]{2,1,0:T(8,128)}) %all-gather.5.cloned.1.call-update) | async-done | bytes 8388624 | tf_op jit(solution)/shard_map/all_gather | solution.py:16
  73.1 18.6 %while.27 = (s32[]{:T(128)}, f32[16,128,128]{2,1,0:T(8,128)}, s32[]{:T(128)}, f32[8,16,128,128]{3,2,1,0:T(8,128)}, s32[]{:T(128)}, /*index=5*/s32[]{:T(128)}) while((s32[]{:T(128)}, f32[16,128,128]{2,1,0:T(8,128)}, s32[]{:T(128)}, f32[8,16,128,128]{3,2,1,0:T(8,128)}, s32[]{:T(128)}, /*index=5*/s32[]{:T(128)}) %tuple.87), condition=%wide.region_1.2_spmd.clone, body=%wide.region_0.1_spmd.clone.sunk | while | flops 786436 | bytes 3145821 | solution.py:23
  73.1 2.4 add_select_fusion.3
  75.5 2.7 add_select_fusion.3
  78.2 2.7 add_select_fusion.3
  80.9 2.7 add_select_fusion.3
  83.6 2.7 add_select_fusion.3
  86.3 2.7 add_select_fusion.3
  89.0 2.7 add_select_fusion.3
  91.7 2.8 convolution_bitcast_fusion.5
  100.8 3.8 multiply_convert_fusion
  104.6 8.9 %gather_fusion.2 = bf16[768,2048]{1,0:T(8,128)(2,1)} fusion(bf16[512,2048]{1,0:T(8,128)(2,1)} %multiply_convert_fusion, s32[1024]{0:T(1024)S(1)} %get-tuple-element.236), kind=kCustom, calls=%fused_computation.2 | custom fusion | bytes 6294528 | tf_op jit(solution)/shard_map/gather | solution.py:148
  113.5 8.2 %gather_fusion = bf16[768,2048]{1,0:T(8,128)(2,1)} fusion(bf16[128,2048]{1,0:T(8,128)(2,1)} %copy.143, s32[1024]{0:T(1024)S(1)} %get-tuple-element.237), kind=kCustom, calls=%fused_computation | custom fusion | bytes 6294528 | tf_op jit(solution)/shard_map/gather | solution.py:141
  121.7 4.3 broadcast_select_fusion
  126.0 76.1 %all_to_all.20 = bf16[32,24,2048]{2,1,0:T(8,128)(2,1)} all-to-all(bf16[32,24,2048]{2,1,0:T(8,128)(2,1)S(1)} %get-tuple-element.231), channel_id=1, replica_groups=mesh['dp'=4,'ctx'=8] {'dp','ctx'}, dimensions={0} | all-to-all | bytes 6291456 | tf_op jit(solution)/shard_map/all_to_all | solution.py:92
  202.1 3.8 all-to-all-start.2
  205.9 7.0 %fusion.4 = f32[768,768]{1,0:T(8,128)} fusion(bf16[768,2048]{1,0:T(8,128)(2,1)} %bitcast.170, bf16[1,2048,768]{2,1,0:T(8,128)(2,1)} %param.23), kind=kOutput, calls=%fused_computation.20 | convolution fusion | flops 2415919104 | bytes 8650752 | tf_op jit(solution)/shard_map/dot_general | solution.py:46
  212.9 4.0 fusion.8
  216.9 60.4 %all-to-all-done.2 = bf16[32,24,2048]{2,1,0:T(8,128)(2,1)} async-done(((bf16[32,24,2048]{2,1,0:T(8,128)(2,1)}), bf16[32,24,2048]{2,1,0:T(8,128)(2,1)}, u32[]{:S(2)}, u32[]{:S(2)}) %all-to-all-start.2) | async-done | bytes 3145760 | tf_op jit(solution)/shard_map/all_to_all | solution.py:92
  277.3 7.9 %multiply_convert_fusion.1 = (bf16[768,768]{1,0:T(8,128)(2,1)S(1)}, bf16[768,768]{1,0:T(8,128)(2,1)S(1)}, bf16[768,768]{1,0:T(8,128)(2,1)}) fusion(f32[768,768]{1,0:T(8,128)} %fusion.8, f32[768,768]{1,0:T(8,128)} %fusion.4, bf16[768,2048]{1,0:T(8,128)(2,1)} %bitcast.23, bf16[1,768,2048]{2,1,0:T(8,128)(2,1)S(1)} %copy-done), kind=kOutput, calls=%fused_computation.32 | convolution fusion | flops 2425356288 | bytes 14548992 | tf_op jit(solution)/shard_map/dot_general | solution.py:56
  285.2 2.6 fusion.6
  288.0 4.0 add_convert_fusion
  291.9 4.0 all-to-all-start.3
  296.0 5.2 convolution_convert_fusion.3
  301.2 66.2 %all-to-all-done.3 = bf16[32,24,2048]{2,1,0:T(8,128)(2,1)} async-done(((bf16[32,24,2048]{2,1,0:T(8,128)(2,1)}), bf16[32,24,2048]{2,1,0:T(8,128)(2,1)}, u32[]{:S(2)}, u32[]{:S(2)}) %all-to-all-start.3) | async-done | bytes 3145760 | tf_op jit(solution)/shard_map/all_to_all | solution.py:92
  367.4 4.0 all-to-all-start.1
  371.7 7.5 %gather_fusion.3 = bf16[512,2048]{1,0:T(8,128)(2,1)} fusion(bf16[768,2048]{1,0:T(8,128)(2,1)} %bitcast.25, s32[1024]{0:T(1024)S(1)} %pad_clamp_fusion.1), kind=kCustom, calls=%fused_computation.3 | custom fusion | bytes 4196352 | tf_op jit(solution)/shard_map/gather | solution.py:167
  379.2 4.7 reshape.283
  384.0 59.0 %all-to-all-done.1 = bf16[32,24,2048]{2,1,0:T(8,128)(2,1)} async-done(((bf16[32,24,2048]{2,1,0:T(8,128)(2,1)}), bf16[32,24,2048]{2,1,0:T(8,128)(2,1)}, u32[]{:S(2)}, u32[]{:S(2)}) %all-to-all-start.1) | async-done | bytes 3145760 | tf_op jit(solution)/shard_map/all_to_all | solution.py:92
  442.9 7.5 %gather_fusion.1 = bf16[512,2048]{1,0:T(8,128)(2,1)} fusion(bf16[768,2048]{1,0:T(8,128)(2,1)} %bitcast.18, s32[1024]{0:T(1024)S(1)} %pad_clamp_fusion.1), kind=kCustom, calls=%fused_computation.1 | custom fusion | bytes 4196352 | tf_op jit(solution)/shard_map/gather | solution.py:163
  450.5 4.8 reshape.279
  455.2 11.2 %multiply_reduce_fusion = (f32[128,4]{1,0:T(8,128)S(1)}, f32[128,2048]{1,0:T(8,128)}, f32[128,2048]{1,0:T(8,128)}) fusion(f32[128,4,2048]{2,1,0:T(4,128)} %reshape.279, f32[128,2048]{1,0:T(8,128)} %copy-done.4, f32[128,4]{1,0:T(8,128)S(1)} %copy.138, f32[128,4,2048]{2,1,0:T(4,128)} %reshape.283), kind=kLoop, calls=%fused_computation.8 | loop fusion | flops 5766656 | bytes 11538432 | tf_op jit(solution)/shard_map/reduce_sum | solution.py:166
  466.5 2.4 fusion.49
  468.9 3.0 convolution_add_fusion
  471.9 2.5 copy.148
  476.3 2.7 divide_convert_fusion
  479.1 2.3 fusion.21
  485.8 2.5 copy.144
  488.3 6.7 %fusion.10 = bf16[1,2048,768]{2,1,0:T(8,128)(2,1)} fusion(bf16[768,2048]{1,0:T(8,128)(2,1)} %bitcast.171, bf16[768,768]{1,0:T(8,128)(2,1)} %copy-done.22), kind=kOutput, calls=%fused_computation.28 | convolution fusion | flops 2417491968 | bytes 7471104 | tf_op jit(solution)/shard_map/dot_general | solution.py:62
  495.1 4.1 fusion.11
  499.1 6.1 fusion.12
  509.8 2.5 fusion.48
  512.3 2.5 fusion.22
  514.7 17.4 %all-reduce.3.cloned.1.call-done = f32[2048,32]{0,1:T(8,128)} async-done(((f32[2048,32]{0,1:T(8,128)}), f32[2048,32]{0,1:T(8,128)}) %all-reduce.3.cloned.1.call-update) | async-done | bytes 262160 | tf_op jit(solution)/shard_map/psum | solution.py:173
  532.1 38.2 %all-gather.7.cloned.1.call-done = bf16[128,128,128]{2,1,0:T(8,128)(2,1)} async-done(((bf16[16,128,128]{2,1,0:T(8,128)(2,1)}), bf16[128,128,128]{2,1,0:T(8,128)(2,1)}) %all-gather.7.cloned.1.call-update) | async-done | bytes 4194320 | tf_op jit(solution)/shard_map/all_gather | solution.py:30
  571.4 17.3 %while.26 = (s32[]{:T(128)}, f32[16,128,128]{2,1,0:T(8,128)}, s32[]{:T(128)}, bf16[8,16,128,128]{3,2,1,0:T(8,128)(2,1)}, s32[]{:T(128)}, /*index=5*/s32[]{:T(128)}, s32[]{:T(128)}, s32[]{:T(128)}) while((s32[]{:T(128)}, f32[16,128,128]{2,1,0:T(8,128)}, s32[]{:T(128)}, bf16[8,16,128,128]{3,2,1,0:T(8,128)(2,1)}, s32[]{:T(128)}, ...), condition=%wide.region_16.17_spmd, body=%wide.region_15.16_spmd.sunk | while | flops 524294 | bytes 2621575 | solution.py:37
  571.4 2.5 convert_add_fusion.2
  573.8 2.5 convert_add_fusion.2
  576.3 2.5 convert_add_fusion.2
  578.8 2.5 convert_add_fusion.2
  581.3 2.5 convert_add_fusion.2
  583.7 2.5 convert_add_fusion.2
  586.2 2.5 convert_add_fusion.2
  588.7 3.7 convolution_bitcast_fusion.3
  592.4 2.9 fusion.16
  597.3 2.7 fusion.20
  602.1 5.8 all-reduce.5.cloned.1.call-done
  (110 shorter events, 32.8 us)
Async XLA Ops:
  7.2 270.2 %copy-start = (bf16[1,768,2048]{2,1,0:T(8,128)(2,1)S(1)}, bf16[1,768,2048]{2,1,0:T(8,128)(2,1)}, u32[]{:S(2)}) copy-start(bf16[1,768,2048]{2,1,0:T(8,128)(2,1)} %param.24) | copy-start | bytes 9437188
  7.2 65.9 %all-gather.5.cloned.1.call-start = ((), (), s32[]{:S(2)}) async-start(), calls=%async_computation.6 | async-start | bytes 9437184 | tf_op jit(solution)/shard_map/all_gather | solution.py:16
  7.2 8.7 %copy-start.18 = (s32[1,128,4]{1,2,0:T(4,128)S(1)}, s32[1,128,4]{1,2,0:T(4,128)}, u32[]{:S(2)}) copy-start(s32[1,128,4]{1,2,0:T(4,128)} %param.21) | copy-start | bytes 6148
  12.7 0.8 copy-start.6
  19.3 1.0 copy-start.4
  91.7 2.8 copy-start.7
  91.7 2.8 copy-start.15
  91.7 4.3 copy-start.17
  94.5 4.7 copy-start.16
  95.1 1.0 copy-start.3
  202.1 75.2 %all-to-all-start.2 = ((bf16[32,24,2048]{2,1,0:T(8,128)(2,1)}), bf16[32,24,2048]{2,1,0:T(8,128)(2,1)}, u32[]{:S(2)}, u32[]{:S(2)}) async-start(bf16[32,24,2048]{2,1,0:T(8,128)(2,1)} %get-tuple-element.230), calls=%async_computation.2 | async-start | bytes 6291456 | tf_op jit(solution)/shard_map/all_to_all | solution.py:92
  205.9 7.0 %copy-start.12 = (bf16[32,24,2048]{2,1,0:T(8,128)(2,1)S(1)}, bf16[32,24,2048]{2,1,0:T(8,128)(2,1)}, u32[]{:S(2)}) copy-start(bf16[32,24,2048]{2,1,0:T(8,128)(2,1)} %all_to_all.20) | copy-start | bytes 9437188
  205.9 7.0 %copy-start.19 = (bf16[1,2048,768]{2,1,0:T(8,128)(2,1)S(1)}, bf16[1,2048,768]{2,1,0:T(8,128)(2,1)}, u32[]{:S(2)}) copy-start(bf16[1,2048,768]{2,1,0:T(8,128)(2,1)} %param.22) | copy-start | bytes 9437188
  277.3 7.9 %copy-start.20 = (bf16[1,2048,768]{2,1,0:T(8,128)(2,1)S(1)}, bf16[1,2048,768]{2,1,0:T(8,128)(2,1)}, u32[]{:S(2)}) copy-start(bf16[1,2048,768]{2,1,0:T(8,128)(2,1)} %param.22) | copy-start | bytes 9437188
  285.2 2.7 copy-start.22
  285.2 2.7 copy-start.24
  285.2 2.7 copy-start.21
  291.9 75.5 %all-to-all-start.3 = ((bf16[32,24,2048]{2,1,0:T(8,128)(2,1)}), bf16[32,24,2048]{2,1,0:T(8,128)(2,1)}, u32[]{:S(2)}, u32[]{:S(2)}) async-start(bf16[32,24,2048]{2,1,0:T(8,128)(2,1)} %bitcast.175), calls=%async_computation.3 | async-start | bytes 6291456 | tf_op jit(solution)/shard_map/all_to_all | solution.py:92
  367.4 75.5 %all-to-all-start.1 = ((bf16[32,24,2048]{2,1,0:T(8,128)(2,1)}), bf16[32,24,2048]{2,1,0:T(8,128)(2,1)}, u32[]{:S(2)}, u32[]{:S(2)}) async-start(bf16[32,24,2048]{2,1,0:T(8,128)(2,1)} %bitcast.174), calls=%async_computation.1 | async-start | bytes 6291456 | tf_op jit(solution)/shard_map/all_to_all | solution.py:92
  371.5 160.6 %all-reduce.3.cloned.1.call-start = ((), (), s32[]{:S(2)}) async-start(), calls=%async_computation.4 | async-start | bytes 524288 | tf_op jit(solution)/shard_map/psum | solution.py:173
  479.0 91.2 %all-gather.7.cloned.1.call-start = ((), (), s32[]{:S(2)}) async-start(), calls=%async_computation.7 | async-start | bytes 4718592 | tf_op jit(solution)/shard_map/all_gather | solution.py:30
  483.5 124.4 %all-reduce.5.cloned.1.call-start = ((), (), s32[]{:S(2)}) async-start(), calls=%async_computation.5 | async-start | bytes 524288 | tf_op jit(solution)/shard_map/psum | solution.py:173
  488.3 6.7 %copy-start.13 = (bf16[32,24,2048]{2,1,0:T(8,128)(2,1)S(1)}, bf16[32,24,2048]{2,1,0:T(8,128)(2,1)}, u32[]{:S(2)}) copy-start(bf16[32,24,2048]{2,1,0:T(8,128)(2,1)} %all_to_all.20) | copy-start | bytes 9437188
  488.3 6.7 %copy-start.25 = (bf16[768,768]{1,0:T(8,128)(2,1)S(1)}, bf16[768,768]{1,0:T(8,128)(2,1)}, u32[]{:S(2)}) copy-start(bf16[768,768]{1,0:T(8,128)(2,1)} %copy-done.24) | copy-start | bytes 3538948
  495.0 4.1 copy-start.23
  499.1 6.1 copy-start.5
  499.1 6.1 copy-start.8
  499.1 6.6 %copy-start.2 = (f32[16,128,128]{2,1,0:T(8,128)S(1)}, f32[16,128,128]{2,1,0:T(8,128)}, u32[]{:S(2)}) copy-start(f32[16,128,128]{2,1,0:T(8,128)} %get-tuple-element.143) | copy-start | bytes 3145732
  499.1 6.6 %copy-start.10 = (f32[1,16,128,128]{3,2,1,0:T(8,128)S(1)}, f32[1,16,128,128]{3,2,1,0:T(8,128)}, u32[]{:S(2)}) copy-start(f32[1,16,128,128]{3,2,1,0:T(8,128)} %param.18) | copy-start | bytes 3145732
  505.2 1.2 copy-start.9
  505.8 2.0 copy-start.14
  588.7 3.7 copy-start.1
  588.7 3.7 copy-start.11
Sparse Core Ops, SparseCore 0:
  16.0 57.0 all-gather.4
  479.2 52.8 all-reduce.2
  534.1 36.0 all-gather.6
  572.5 35.2 all-reduce.4
